TPU v7x, 128 devices: a whole 4x4x4 slice. The times are simulated.
128 devices in a mesh: dom: 64 (over x, z, y), batch: 2 (over core).
Axes of the slice: x: 4, y: 4, z: 4, core: 2. Of those that a mesh axis runs over, the one named last changes fastest.
Arguments:
- features: bfloat16 [4, 65536, 512], P('batch', 'dom'), may hold values from -6 to 6
- tile_vals: bfloat16 [2048, 128, 128], P('dom'), may hold values from -0.25 to 0.25
- tile_row: int32 [2048], P('dom'), may hold values from 0 to 7
- tile_col: int32 [2048], P('dom'), may hold values from 0 to 11
- send_next: int32 [128], P('dom'), may hold values from 0 to 7
- send_prev: int32 [128], P('dom'), may hold values from 0 to 7
- cluster: int32 [65536], P('dom'), may hold values from 0 to 1023, as said below
- cotangent: bfloat16 [4, 65536, 512], P('batch', 'dom'), may hold values from -6 to 6
- self_weight: bfloat16 [512, 512], replicated, may hold values from -0.25 to 0.25
- neighbour_weight: bfloat16 [512, 512], replicated, may hold values from -0.25 to 0.25
- w_coarse: bfloat16 [512, 512], replicated, may hold values from -0.25 to 0.25
Outputs:
- output: bfloat16 [4, 65536, 512], P('batch', 'dom')
- self_weight_gradient: float32 [512, 512], replicated
- neighbour_weight_gradient: float32 [512, 512], replicated
- grad_coarse: float32 [512, 512], replicated
Inputs may be any that keep to these rules, and one draw needn't show every extreme that they name: Within each pair of partitions 2m, 2m + 1, every cluster number names exactly two of the pair's 2 * 1024 nodes.
All inputs are finite; a program needn't handle non-finite values.
Results may differ from a plain program's by a relative error of at most 0.012.
Values may be sent and summed in bfloat16 or wider, within the bound.
A program may use at most 128 MiB of HBM per device.

v0:
```python
import math
import jax
import jax.numpy as jnp
from jax import lax
from jax.sharding import PartitionSpec as P


def shifted(x, axis, by):
    length = lax.axis_size(axis)
    pairs = [(i, i + by) for i in range(length) if 0 <= i + by < length]
    return lax.ppermute(x, axis, pairs)


def partner(value, axis, distance):
    mask = 2**distance
    pairs = [(source, source ^ mask) for source in range(lax.axis_size(axis))]
    return lax.ppermute(value, axis, pairs)


def dsilu(value):
    sig = jax.nn.sigmoid(value)
    return sig * (1.0 + value * (1.0 - sig))


def member_table(labels, count):
    return (labels[None, :] == jnp.arange(count, dtype=jnp.int32)[:, None]).astype(jnp.bfloat16)


def pooling(rows, table):
    return jnp.einsum("cn,snd->scd", table, rows, preferred_element_type=jnp.float32)


def lookup(coarse_rows, table):
    return jnp.einsum("cn,scd->snd", table, coarse_rows, preferred_element_type=jnp.float32)


def pick_blocks(labels, count, tiled):
    table = (labels[:, None] == jnp.arange(count, dtype=jnp.int32)[None, :]).astype(jnp.bfloat16)
    return jnp.einsum("tb,sbjd->stjd", table, tiled, preferred_element_type=jnp.float32).astype(
        jnp.bfloat16
    )


def local(
    features,
    tile_vals,
    tile_row,
    tile_col,
    send_next,
    send_prev,
    cluster,
    cotangent,
    self_weight,
    neighbour_weight,
    w_coarse,
):
    scen, nodes, width = features.shape
    side = tile_vals.shape[1]
    blocks = nodes // side
    tiled = features.reshape(scen, blocks, side, width)
    to_next = pick_blocks(send_next, blocks, tiled)
    to_prev = pick_blocks(send_prev, blocks, tiled)
    got_prev = shifted(to_next, "dom", 1)
    got_next = shifted(to_prev, "dom", -1)
    extended = jnp.concatenate([tiled, got_prev, got_next], axis=1)
    picked = pick_blocks(tile_col, extended.shape[1], extended)
    terms = jnp.einsum("tij,stjd->stid", tile_vals, picked, preferred_element_type=jnp.float32)
    rowhot = (tile_row[None, :] == jnp.arange(blocks, dtype=jnp.int32)[:, None]).astype(jnp.float32)
    summed = jnp.einsum("rt,stid->srid", rowhot, terms, precision=lax.Precision.HIGHEST)
    neighbour_total = summed.reshape(scen, nodes, width).astype(jnp.bfloat16)
    preactivation = jnp.einsum(
        "jkb,bt->jkt", features, self_weight, preferred_element_type=jnp.float32
    )
    preactivation = preactivation + jnp.einsum(
        "jkb,bt->jkt", neighbour_total, neighbour_weight, preferred_element_type=jnp.float32
    )
    hidden = jax.nn.silu(preactivation).astype(jnp.bfloat16)
    table = member_table(cluster, nodes)
    parity = lax.axis_index("dom") % 2
    half = nodes // 2
    own_start = parity * half

    def owned(array):
        return lax.dynamic_slice_in_dim(array, own_start, half, 1)

    partial_value = pooling(hidden, table)
    grad_partial = pooling(cotangent, table)
    partner_sums = partner(partial_value.astype(jnp.bfloat16), "dom", 0).astype(partial_value.dtype)
    coarse = (0.5 * (partial_value + partner_sums)).astype(jnp.bfloat16)
    act = jnp.einsum("skd,de->ske", coarse, w_coarse, preferred_element_type=jnp.float32)
    lifted = jax.nn.silu(act).astype(jnp.bfloat16)
    grad_lift = grad_partial + partner(grad_partial.astype(jnp.bfloat16), "dom", 0).astype(
        grad_partial.dtype
    )
    grad_act = (grad_lift * dsilu(act)).astype(jnp.bfloat16)
    term_coarse = jnp.einsum(
        "skd,ske->de", owned(coarse), owned(grad_act), preferred_element_type=jnp.float32
    )
    grad_down = jnp.einsum(
        "ske,de->skd", grad_act, w_coarse, preferred_element_type=jnp.float32
    ).astype(jnp.bfloat16)
    spread = lookup(lifted, table)
    output = (hidden.astype(jnp.float32) + spread).astype(jnp.bfloat16)
    back = lookup(grad_down, table)
    grad_hidden = cotangent.astype(jnp.float32) + 0.5 * back
    preactivation_gradient = (grad_hidden * dsilu(preactivation)).astype(jnp.bfloat16)
    self_contribution = jnp.einsum(
        "btv,btq->vq", features, preactivation_gradient, preferred_element_type=jnp.float32
    )
    neighbour_contribution = jnp.einsum(
        "btv,btq->vq", neighbour_total, preactivation_gradient, preferred_element_type=jnp.float32
    )
    totals = lax.psum((self_contribution, neighbour_contribution, term_coarse), ("dom", "batch"))
    gradient_scale = 1.0 / math.sqrt(scen * lax.axis_size("batch") * nodes * lax.axis_size("dom"))
    return (
        output,
        totals[0] * gradient_scale,
        totals[1] * gradient_scale,
        totals[2] * gradient_scale,
    )


def solution(mesh):
    in_specs = (
        P("batch", "dom", None),
        P("dom", None, None),
        P("dom"),
        P("dom"),
        P("dom"),
        P("dom"),
        P("dom"),
        P("batch", "dom", None),
        P(),
        P(),
        P(),
    )
    out_specs = (P("batch", "dom", None), P(), P(), P())
    return jax.shard_map(local, mesh=mesh, in_specs=in_specs, out_specs=out_specs, check_vma=False)
```

profile of v0, /device:TPU:1, one launch (start us, length us, event | category | flops | bytes accessed | tf_op | source)
XLA Modules:
  0.0 384.3 jit_solution(13734323582045857980)
XLA Ops:
  7.2 3.2 fusion.35
  10.5 4.1 %collective-permute-start = (bf16[2,2,128,512]{3,1,2,0:T(2,128)(2,1)S(1)}, bf16[2,2,128,512]{3,1,2,0:T(2,128)(2,1)S(1)}, u32[]{:S(2)}, u32[]{:S(2)}) collective-permute-start(bf16[2,2,128,512]{3,1,2,0:T(2,128)(2,1)S(1)} %fusion.35), channel_id=1, source_target_pairs={{0,2},{2,4},{4,6},{6,8},{8,10},{10,12},{12,14},{14,16},{16,18},{18... | collective-permute-start | bytes 1572872 | tf_op jit(solution)/shard_map/ppermute | solution.py:11
  14.5 3.1 fusion.36
  20.1 3.3 fusion.45
  23.4 1.7 collective-permute-done
  25.1 6.9 %collective-permute-done.1 = bf16[2,2,128,512]{3,1,2,0:T(2,128)(2,1)S(1)} collective-permute-done((bf16[2,2,128,512]{3,1,2,0:T(2,128)(2,1)S(1)}, bf16[2,2,128,512]{3,1,2,0:T(2,128)(2,1)S(1)}, u32[]{:S(2)}, u32[]{:S(2)}) %collective-permute-start.1) | collective-permute-done | bytes 524320 | tf_op jit(solution)/shard_map/ppermute | solution.py:11
  32.0 5.3 %convert_bitcast_fusion = bf16[2,32,128,512]{3,1,2,0:T(8,128)(2,1)} fusion(bf16[2,2,128,512]{3,1,2,0:T(2,128)(2,1)S(1)} %collective-permute-done.1, bf16[2,2,128,512]{3,1,2,0:T(2,128)(2,1)S(1)} %collective-permute-done, bf16[2,8,128,512]{3,1,2,0:T(8,128)(2,1)S(1)} %copy.58, s32[32]{0:T(128)S(1)} %copy-done.15), kind=kOutput, calls=%fused_computation.2 | convolution fusion | flops 114295168 | bytes 11534464 | tf_op jit(solution)/shard_map/tb,sbjd->stjd/dot_general | solution.py:39
  37.3 18.5 %convolution_bitcast_fusion = f32[2,32,128,512]{2,3,0,1:T(8,128)} fusion(bf16[2,32,128,512]{3,1,2,0:T(8,128)(2,1)} %convert_bitcast_fusion, bf16[32,128,128]{2,1,0:T(8,128)(2,1)S(1)} %copy-done), kind=kOutput, calls=%fused_computation | convolution fusion | flops 1073741824 | bytes 26214400 | tf_op jit(solution)/shard_map/tij,stjd->stid/dot_general | solution.py:67
  55.8 20.1 %copy.60 = f32[2,32,128,512]{3,1,2,0:T(8,128)} copy(f32[2,32,128,512]{2,3,0,1:T(8,128)} %convolution_bitcast_fusion) | data formatting | bytes 33554432 | tf_op jit(solution)/shard_map/tij,stjd->stid/transpose | solution.py:67
  75.9 9.2 %convert_bitcast_fusion.1 = bf16[2,8,128,512]{3,1,2,0:T(8,128)(2,1)S(1)} fusion(f32[2,32,128,512]{3,1,2,0:T(8,128)} %copy.60, s32[32]{0:T(128)S(1)} %copy-done.11), kind=kOutput, calls=%fused_computation.37 | convolution fusion | flops 403702016 | bytes 18874496 | tf_op jit(solution)/shard_map/rt,stid->srid/dot_general | solution.py:69
  89.3 5.5 %bitcast_convert_fusion.1 = (bf16[2,1024,512]{1,2,0:T(8,128)(2,1)}, f32[2,512,1024]{2,1,0:T(8,128)}) fusion(s32[1024]{0:T(1024)S(1)} %copy-done.14, f32[2,1024,512]{2,1,0:T(8,128)S(1)} %convolution_add_fusion), kind=kOutput, calls=%fused_computation.18 | convolution fusion | flops 2154823680 | bytes 10489856 | tf_op jit(solution)/shard_map/cn,snd->scd/dot_general | solution.py:30
  96.1 5.0 %bitcast_convert_fusion = (bf16[2,1024,512]{2,1,0:T(8,128)(2,1)}, f32[1024,2,512]{2,0,1:T(8,128)}) fusion(bf16[2,1024,512]{2,1,0:T(8,128)(2,1)S(1)} %copy-done.12, s32[1024]{0:T(1024)S(1)} %copy-done.14), kind=kOutput, calls=%fused_computation.12 | convolution fusion | flops 2149580800 | bytes 8392704 | tf_op jit(solution)/shard_map/cn,snd->scd/dot_general | solution.py:30
  101.5 38.9 %collective-permute-done.2 = bf16[2,1024,512]{1,2,0:T(8,128)(2,1)} collective-permute-done((bf16[2,1024,512]{1,2,0:T(8,128)(2,1)}, bf16[2,1024,512]{1,2,0:T(8,128)(2,1)}, u32[]{:S(2)}, u32[]{:S(2)}) %collective-permute-start.2) | collective-permute-done | bytes 2097184 | tf_op jit(solution)/shard_map/ppermute | solution.py:17
  140.4 3.8 fusion.12
  144.2 41.1 %collective-permute-done.3 = bf16[2,1024,512]{2,1,0:T(8,128)(2,1)} collective-permute-done((bf16[2,1024,512]{2,1,0:T(8,128)(2,1)}, bf16[2,1024,512]{2,1,0:T(8,128)(2,1)}, u32[]{:S(2)}, u32[]{:S(2)}) %collective-permute-start.3) | collective-permute-done | bytes 2097184 | tf_op jit(solution)/shard_map/ppermute | solution.py:17
  185.3 6.8 %fusion.9 = (bf16[2,1024,512]{2,1,0:T(8,128)(2,1)}, f32[2,1024,512]{2,1,0:T(8,128)}) fusion(f32[1024,2,512]{2,0,1:T(8,128)S(1)} %copy-done.17, bf16[2,1024,512]{2,1,0:T(8,128)(2,1)} %collective-permute-done.3, bf16[2,1024,512]{1,2,0:T(8,128)(2,1)S(1)} %fusion.12, bf16[512,512]{1,0:T(8,128)(2,1)S(1)} %copy-done.13), kind=kOutput, calls=%fused_computation.14 | convolution fusion | flops 1085276160 | bytes 15204352 | tf_op jit(solution)/shard_map/skd,de->ske/dot_general | solution.py:90
  192.1 8.1 %fusion.7 = bf16[2,1024,512]{2,1,0:T(8,128)(2,1)} fusion(f32[2,1024,512]{2,1,0:T(8,128)} %copy-done.5, bf16[2,1024,512]{2,1,0:T(8,128)(2,1)} %param.18, s32[1024]{0:T(1024)S(1)} %copy-done.14, bf16[2,1024,512]{2,1,0:T(8,128)(2,1)} %get-tuple-element.27, bf16[512,512]{1,0:T(8,128)(2,1)S(1)} %copy-done.13), kind=kOutput, calls=%fused_computation.10 | convolution fusion | flops 3235905536 | bytes 11014144 | tf_op jit(solution)/shard_map/cn,scd->snd/dot_general | solution.py:34
  200.2 4.6 %convolution_bitcast_fusion.2 = f32[512,512]{0,1:T(8,128)} fusion(bf16[2,1024,512]{2,1,0:T(8,128)(2,1)} %bitcast.111, bf16[2,1024,512]{2,1,0:T(8,128)(2,1)} %fusion.7), kind=kOutput, calls=%fused_computation.40 | convolution fusion | flops 1073741824 | bytes 5242880 | tf_op jit(solution)/shard_map/btv,btq->vq/dot_general | solution.py:110
  204.8 2.2 convolution_bitcast_fusion.3
  207.0 1.7 convolution_bitcast_fusion.1
  208.8 8.0 %fusion.10 = bf16[2,1024,512]{2,1,0:T(8,128)(2,1)} fusion(s32[1024]{0:T(1024)S(1)} %copy-done.14, f32[2,1024,512]{2,1,0:T(8,128)} %get-tuple-element.28, f32[2,1024,512]{2,1,0:T(8,128)} %copy-done.5), kind=kOutput, calls=%fused_computation.16 | convolution fusion | flops 2162163712 | bytes 10489856 | tf_op jit(solution)/shard_map/cn,scd->snd/dot_general | solution.py:34
  216.8 153.4 %all-reduce.3.cloned.1.call-done = (f32[512,512]{0,1:T(8,128)}, f32[512,512]{0,1:T(8,128)}, f32[512,512]{0,1:T(8,128)}) async-done(((f32[512,512]{0,1:T(8,128)}, f32[512,512]{0,1:T(8,128)}, f32[512,512]{0,1:T(8,128)}), (f32[512,512]{0,1:T(8,128)}, f32[512,512]{0,1:T(8,128)}, f32[512,512]{0,1:T(8,128)})) %all-reduce.3.cloned.1.call-update) | async-done | bytes 3145744 | tf_op jit(solution)/shard_map/psum | solution.py:113
  370.2 1.8 broadcast_multiply_fusion
  374.6 1.3 broadcast_multiply_fusion.2
  (47 shorter events, 12.3 us)
Async XLA Ops:
  7.2 30.1 %copy-start = (bf16[32,128,128]{2,1,0:T(8,128)(2,1)S(1)}, bf16[32,128,128]{2,1,0:T(8,128)(2,1)}, u32[]{:S(2)}) copy-start(bf16[32,128,128]{2,1,0:T(8,128)(2,1)} %param.12) | copy-start | bytes 3145732
  7.2 11.7 %copy-start.2 = (bf16[2,1024,512]{2,1,0:T(8,128)(2,1)S(1)}, bf16[2,1024,512]{2,1,0:T(8,128)(2,1)}, u32[]{:S(2)}) copy-start(bf16[2,1024,512]{2,1,0:T(8,128)(2,1)} %param.11) | copy-start | bytes 6291460
  7.2 363.0 %all-reduce.3.cloned.1.call-start = ((), (), s32[]{:S(2)}) async-start(), calls=%async_computation | async-start | bytes 6291456 | tf_op jit(solution)/shard_map/psum | solution.py:113
  7.2 12.8 %copy-start.9 = (bf16[512,512]{1,0:T(8,128)(2,1)S(1)}, bf16[512,512]{1,0:T(8,128)(2,1)}, u32[]{:S(2)}) copy-start(bf16[512,512]{1,0:T(8,128)(2,1)} %param.19) | copy-start | bytes 1572868
  10.5 14.6 %collective-permute-start = (bf16[2,2,128,512]{3,1,2,0:T(2,128)(2,1)S(1)}, bf16[2,2,128,512]{3,1,2,0:T(2,128)(2,1)S(1)}, u32[]{:S(2)}, u32[]{:S(2)}) collective-permute-start(bf16[2,2,128,512]{3,1,2,0:T(2,128)(2,1)S(1)} %fusion.35), channel_id=1, source_target_pairs={{0,2},{2,4},{4,6},{6,8},{8,10},{10,12},{12,14},{14,16},{16,18},{18... | collective-permute-start | bytes 1572872 | tf_op jit(solution)/shard_map/ppermute | solution.py:11
  17.6 14.4 %collective-permute-start.1 = (bf16[2,2,128,512]{3,1,2,0:T(2,128)(2,1)S(1)}, bf16[2,2,128,512]{3,1,2,0:T(2,128)(2,1)S(1)}, u32[]{:S(2)}, u32[]{:S(2)}) collective-permute-start(bf16[2,2,128,512]{3,1,2,0:T(2,128)(2,1)S(1)} %fusion.36), channel_id=1, source_target_pairs={{2,0},{4,2},{6,4},{8,6},{10,8},{12,10},{14,12},{16,14},{18,16},{20... | collective-permute-start | bytes 1572872 | tf_op jit(solution)/shard_map/ppermute | solution.py:11
  20.1 11.9 %copy-start.15 = (s32[32]{0:T(128)S(1)}, s32[32]{0:T(128)}, u32[]{:S(2)}) copy-start(s32[32]{0:T(128)} %param.14) | copy-start | bytes 388
  55.8 20.1 %copy-start.11 = (s32[32]{0:T(128)S(1)}, s32[32]{0:T(128)}, u32[]{:S(2)}) copy-start(s32[32]{0:T(128)} %param.13) | copy-start | bytes 388
  75.8 11.3 %copy-start.10 = (bf16[512,512]{1,0:T(8,128)(2,1)S(1)}, bf16[512,512]{1,0:T(8,128)(2,1)}, u32[]{:S(2)}) copy-start(bf16[512,512]{1,0:T(8,128)(2,1)} %param.20) | copy-start | bytes 1572868
  85.1 2.9 copy-start.3
  85.8 1.3 copy-start.4
  88.1 1.3 copy-start.14
  89.3 5.5 %copy-start.5 = (f32[2,1024,512]{2,1,0:T(8,128)}, f32[2,1024,512]{2,1,0:T(8,128)S(1)}, u32[]{:S(2)}) copy-start(f32[2,1024,512]{2,1,0:T(8,128)S(1)} %convolution_add_fusion) | copy-start | bytes 12582916
  89.3 6.8 %copy-start.12 = (bf16[2,1024,512]{2,1,0:T(8,128)(2,1)S(1)}, bf16[2,1024,512]{2,1,0:T(8,128)(2,1)}, u32[]{:S(2)}) copy-start(bf16[2,1024,512]{2,1,0:T(8,128)(2,1)} %param.18) | copy-start | bytes 6291460
  94.8 45.6 %collective-permute-start.2 = (bf16[2,1024,512]{1,2,0:T(8,128)(2,1)}, bf16[2,1024,512]{1,2,0:T(8,128)(2,1)}, u32[]{:S(2)}, u32[]{:S(2)}) collective-permute-start(bf16[2,1024,512]{1,2,0:T(8,128)(2,1)} %get-tuple-element.23), channel_id=1, source_target_pairs={{0,2},{2,0},{4,6},{6,4},{8,10},{10,8},{12,14},{14,12},{16,18},{18,... | collective-permute-start | bytes 6291464 | tf_op jit(solution)/shard_map/ppermute | solution.py:17
  101.1 84.2 %collective-permute-start.3 = (bf16[2,1024,512]{2,1,0:T(8,128)(2,1)}, bf16[2,1024,512]{2,1,0:T(8,128)(2,1)}, u32[]{:S(2)}, u32[]{:S(2)}) collective-permute-start(bf16[2,1024,512]{2,1,0:T(8,128)(2,1)} %get-tuple-element.25), channel_id=1, source_target_pairs={{0,2},{2,0},{4,6},{6,4},{8,10},{10,8},{12,14},{14,12},{16,18},{18,... | collective-permute-start | bytes 6291464 | tf_op jit(solution)/shard_map/ppermute | solution.py:17
  140.4 44.9 %copy-start.13 = (bf16[512,512]{1,0:T(8,128)(2,1)S(1)}, bf16[512,512]{1,0:T(8,128)(2,1)}, u32[]{:S(2)}) copy-start(bf16[512,512]{1,0:T(8,128)(2,1)} %param.21) | copy-start | bytes 1572868
  140.4 44.9 %copy-start.17 = (f32[1024,2,512]{2,0,1:T(8,128)S(1)}, f32[1024,2,512]{2,0,1:T(8,128)}, u32[]{:S(2)}) copy-start(f32[1024,2,512]{2,0,1:T(8,128)} %get-tuple-element.26) | copy-start | bytes 12582916
  144.2 47.9 %copy-start.7 = (bf16[2,1024,512]{1,2,0:T(8,128)(2,1)}, bf16[2,1024,512]{1,2,0:T(8,128)(2,1)S(1)}, u32[]{:S(2)}) copy-start(bf16[2,1024,512]{1,2,0:T(8,128)(2,1)S(1)} %fusion.12) | copy-start | bytes 6291460
  200.2 4.6 %copy-start.6 = (bf16[2,1024,512]{2,1,0:T(8,128)(2,1)S(1)}, bf16[2,1024,512]{2,1,0:T(8,128)(2,1)}, u32[]{:S(2)}) copy-start(bf16[2,1024,512]{2,1,0:T(8,128)(2,1)} %fusion.7) | copy-start | bytes 6291460
  204.8 2.2 copy-start.8
  204.8 2.2 copy-start.16
  371.9 5.3 %copy-start.1 = (bf16[32,128,128]{2,1,0:T(8,128)(2,1)S(1)}, bf16[32,128,128]{2,1,0:T(8,128)(2,1)}, u32[]{:S(2)}) copy-start(bf16[32,128,128]{2,1,0:T(8,128)(2,1)} %param.12) | copy-start | bytes 3145732
Sparse Core Ops, SparseCore 0:
  208.9 161.1 all-reduce.2
where the time goes:
time: 389 us; the launch traced here: 384 us
  waiting for transfers between devices  242 us (62%)
  matrix products  85.8 us (22%)
  local copies, waits for them, and re-layouts  28.1 us (7%)
  between operations  14.5 us (4%)
  starting transfers between devices  7.05 us (2%)
  other arithmetic  6.86 us (2%)
    psum x1, waiting for transfers between devices, local(): lax.psum((self_contribution, neighbour_contribution, term_coarse), ('dom'...  153 us
    ppermute x2, waiting for transfers between devices, partner(): return lax.ppermute(value, axis, pairs)  80 us
    transpose x1, local copies, waits for them, and re-layouts, local(): jnp.einsum('tij,stjd->stid', tile_vals, picked, preferred_element_type=jn...  20.1 us
    dot_general x1, matrix products, local(): jnp.einsum('tij,stjd->stid', tile_vals, picked, preferred_element_type=jn...  18.5 us
    dot_general x2, matrix products, lookup(): jnp.einsum('cn,scd->snd', table, coarse_rows, preferred_element_type=jnp....  16.1 us
    dot_general x3, matrix products, pick_blocks(): jnp.einsum('tb,sbjd->stjd', table, tiled, preferred_element_type=jnp.floa...  11.6 us
    dot_general x2, matrix products, pooling(): jnp.einsum('cn,snd->scd', table, rows, preferred_element_type=jnp.float32)  10.5 us
    dot_general x1, matrix products, local(): jnp.einsum('rt,stid->srid', rowhot, terms, precision=lax.Precision.HIGHEST)  9.25 us
  transfers between devices with their start and end apart: 5, of which 5 were waited for; matrix products, arithmetic and copies ran while one was open for 6% of the time, Pallas kernels for 0%

commit v1 on v0

--- a/solution.py
+++ b/solution.py
@@ -54,6 +54,12 @@
     neighbour_weight,
     w_coarse,
 ):
+
+    def _trace_space(w_in, named_axis, ax_name):
+        for w in (named_axis, ax_name):
+            w_in = jax.lax.psum(w_in, w)
+        return w_in
+
     scen, nodes, width = features.shape
     side = tile_vals.shape[1]
     blocks = nodes // side
@@ -110,7 +116,7 @@
     neighbour_contribution = jnp.einsum(
         "btv,btq->vq", neighbour_total, preactivation_gradient, preferred_element_type=jnp.float32
     )
-    totals = lax.psum((self_contribution, neighbour_contribution, term_coarse), ("dom", "batch"))
+    totals = _trace_space((self_contribution, neighbour_contribution, term_coarse), "batch", "dom")
     gradient_scale = 1.0 / math.sqrt(scen * lax.axis_size("batch") * nodes * lax.axis_size("dom"))
     return (
         output,

time: 389 us -> 408 us (1.049)
  waiting for transfers between devices: 242 us -> 259 us
    psum x1 -> x2, waiting for transfers between devices: 153 us -> 171 us  [_trace_space(): w_in = jax.lax.psum(w_in, w)]
  transfers between devices with their start and end apart: 5 -> 6, of which waited for: 5 -> 6; matrix products, arithmetic and copies ran while one was open for 6% -> 6% of each run, Pallas kernels for 0% -> 0%
where the time goes in v1:
time: 408 us; the launch traced here: 402 us
  waiting for transfers between devices  259 us (63%)
  matrix products  86 us (21%)
  local copies, waits for them, and re-layouts  28.1 us (7%)
  between operations  14.5 us (4%)
  starting transfers between devices  7.26 us (2%)
  other arithmetic  6.86 us (2%)
    psum x2, waiting for transfers between devices, _trace_space(): w_in = jax.lax.psum(w_in, w)  171 us
    ppermute x2, waiting for transfers between devices, partner(): return lax.ppermute(value, axis, pairs)  80.1 us
    transpose x1, local copies, waits for them, and re-layouts, local(): jnp.einsum('tij,stjd->stid', tile_vals, picked, preferred_element_type=jn...  20 us
    dot_general x1, matrix products, local(): jnp.einsum('tij,stjd->stid', tile_vals, picked, preferred_element_type=jn...  18.5 us
    dot_general x2, matrix products, lookup(): jnp.einsum('cn,scd->snd', table, coarse_rows, preferred_element_type=jnp....  16.1 us
    dot_general x3, matrix products, pick_blocks(): jnp.einsum('tb,sbjd->stjd', table, tiled, preferred_element_type=jnp.floa...  11.4 us
    dot_general x2, matrix products, pooling(): jnp.einsum('cn,snd->scd', table, rows, preferred_element_type=jnp.float32)  10.5 us
    dot_general x1, matrix products, local(): jnp.einsum('rt,stid->srid', rowhot, terms, precision=lax.Precision.HIGHEST)  9.57 us
  transfers between devices with their start and end apart: 6, of which 6 were waited for; matrix products, arithmetic and copies ran while one was open for 6% of the time, Pallas kernels for 0%

profile of v1, /device:TPU:1, one launch (start us, length us, event | category | flops | bytes accessed | tf_op | source)
XLA Modules:
  0.0 402.1 jit_solution(16295555400429730939)
XLA Ops:
  7.2 3.2 fusion.35
  10.5 4.1 %collective-permute-start = (bf16[2,2,128,512]{3,1,2,0:T(2,128)(2,1)S(1)}, bf16[2,2,128,512]{3,1,2,0:T(2,128)(2,1)S(1)}, u32[]{:S(2)}, u32[]{:S(2)}) collective-permute-start(bf16[2,2,128,512]{3,1,2,0:T(2,128)(2,1)S(1)} %fusion.35), channel_id=1, source_target_pairs={{0,2},{2,4},{4,6},{6,8},{8,10},{10,12},{12,14},{14,16},{16,18},{18... | collective-permute-start | bytes 1572872 | tf_op jit(solution)/shard_map/ppermute | solution.py:11
  14.5 3.1 fusion.36
  20.1 3.3 fusion.45
  23.4 1.7 collective-permute-done
  25.1 6.9 %collective-permute-done.1 = bf16[2,2,128,512]{3,1,2,0:T(2,128)(2,1)S(1)} collective-permute-done((bf16[2,2,128,512]{3,1,2,0:T(2,128)(2,1)S(1)}, bf16[2,2,128,512]{3,1,2,0:T(2,128)(2,1)S(1)}, u32[]{:S(2)}, u32[]{:S(2)}) %collective-permute-start.1) | collective-permute-done | bytes 524320 | tf_op jit(solution)/shard_map/ppermute | solution.py:11
  32.0 5.1 %convert_bitcast_fusion = bf16[2,32,128,512]{3,1,2,0:T(8,128)(2,1)} fusion(bf16[2,2,128,512]{3,1,2,0:T(2,128)(2,1)S(1)} %collective-permute-done.1, bf16[2,2,128,512]{3,1,2,0:T(2,128)(2,1)S(1)} %collective-permute-done, bf16[2,8,128,512]{3,1,2,0:T(8,128)(2,1)S(1)} %copy.58, s32[32]{0:T(128)S(1)} %copy-done.15), kind=kOutput, calls=%fused_computation.2 | convolution fusion | flops 114295168 | bytes 11534464 | tf_op jit(solution)/shard_map/tb,sbjd->stjd/dot_general | solution.py:39
  37.1 18.5 %convolution_bitcast_fusion = f32[2,32,128,512]{2,3,0,1:T(8,128)} fusion(bf16[2,32,128,512]{3,1,2,0:T(8,128)(2,1)} %convert_bitcast_fusion, bf16[32,128,128]{2,1,0:T(8,128)(2,1)S(1)} %copy-done), kind=kOutput, calls=%fused_computation | convolution fusion | flops 1073741824 | bytes 26214400 | tf_op jit(solution)/shard_map/tij,stjd->stid/dot_general | solution.py:73
  55.6 20.0 %copy.60 = f32[2,32,128,512]{3,1,2,0:T(8,128)} copy(f32[2,32,128,512]{2,3,0,1:T(8,128)} %convolution_bitcast_fusion) | data formatting | bytes 33554432 | tf_op jit(solution)/shard_map/tij,stjd->stid/transpose | solution.py:73
  75.6 9.6 %convert_bitcast_fusion.1 = bf16[2,8,128,512]{3,1,2,0:T(8,128)(2,1)S(1)} fusion(f32[2,32,128,512]{3,1,2,0:T(8,128)} %copy.60, s32[32]{0:T(128)S(1)} %copy-done.11), kind=kOutput, calls=%fused_computation.37 | convolution fusion | flops 403702016 | bytes 18874496 | tf_op jit(solution)/shard_map/rt,stid->srid/dot_general | solution.py:75
  89.4 5.5 %bitcast_convert_fusion.1 = (bf16[2,1024,512]{1,2,0:T(8,128)(2,1)}, f32[2,512,1024]{2,1,0:T(8,128)}) fusion(s32[1024]{0:T(1024)S(1)} %copy-done.14, f32[2,1024,512]{2,1,0:T(8,128)S(1)} %convolution_add_fusion), kind=kOutput, calls=%fused_computation.18 | convolution fusion | flops 2154823680 | bytes 10489856 | tf_op jit(solution)/shard_map/cn,snd->scd/dot_general | solution.py:30
  96.1 5.0 %bitcast_convert_fusion = (bf16[2,1024,512]{2,1,0:T(8,128)(2,1)}, f32[1024,2,512]{2,0,1:T(8,128)}) fusion(bf16[2,1024,512]{2,1,0:T(8,128)(2,1)S(1)} %copy-done.12, s32[1024]{0:T(1024)S(1)} %copy-done.14), kind=kOutput, calls=%fused_computation.12 | convolution fusion | flops 2149580800 | bytes 8392704 | tf_op jit(solution)/shard_map/cn,snd->scd/dot_general | solution.py:30
  101.5 38.9 %collective-permute-done.2 = bf16[2,1024,512]{1,2,0:T(8,128)(2,1)} collective-permute-done((bf16[2,1024,512]{1,2,0:T(8,128)(2,1)}, bf16[2,1024,512]{1,2,0:T(8,128)(2,1)}, u32[]{:S(2)}, u32[]{:S(2)}) %collective-permute-start.2) | collective-permute-done | bytes 2097184 | tf_op jit(solution)/shard_map/ppermute | solution.py:17
  140.4 3.8 fusion.12
  144.2 41.1 %collective-permute-done.3 = bf16[2,1024,512]{2,1,0:T(8,128)(2,1)} collective-permute-done((bf16[2,1024,512]{2,1,0:T(8,128)(2,1)}, bf16[2,1024,512]{2,1,0:T(8,128)(2,1)}, u32[]{:S(2)}, u32[]{:S(2)}) %collective-permute-start.3) | collective-permute-done | bytes 2097184 | tf_op jit(solution)/shard_map/ppermute | solution.py:17
  185.4 6.7 %fusion.9 = (bf16[2,1024,512]{2,1,0:T(8,128)(2,1)}, f32[2,1024,512]{2,1,0:T(8,128)}) fusion(f32[1024,2,512]{2,0,1:T(8,128)S(1)} %copy-done.17, bf16[2,1024,512]{2,1,0:T(8,128)(2,1)} %collective-permute-done.3, bf16[2,1024,512]{1,2,0:T(8,128)(2,1)S(1)} %fusion.12, bf16[512,512]{1,0:T(8,128)(2,1)S(1)} %copy-done.13), kind=kOutput, calls=%fused_computation.14 | convolution fusion | flops 1085276160 | bytes 15204352 | tf_op jit(solution)/shard_map/skd,de->ske/dot_general | solution.py:96
  192.1 8.1 %fusion.7 = bf16[2,1024,512]{2,1,0:T(8,128)(2,1)} fusion(f32[2,1024,512]{2,1,0:T(8,128)} %copy-done.5, bf16[2,1024,512]{2,1,0:T(8,128)(2,1)} %param.18, s32[1024]{0:T(1024)S(1)} %copy-done.14, bf16[2,1024,512]{2,1,0:T(8,128)(2,1)} %get-tuple-element.30, bf16[512,512]{1,0:T(8,128)(2,1)S(1)} %copy-done.13), kind=kOutput, calls=%fused_computation.10 | convolution fusion | flops 3235905536 | bytes 11014144 | tf_op jit(solution)/shard_map/cn,scd->snd/dot_general | solution.py:34
  200.2 4.6 %convolution_bitcast_fusion.2 = f32[512,512]{0,1:T(8,128)} fusion(bf16[2,1024,512]{2,1,0:T(8,128)(2,1)} %bitcast.111, bf16[2,1024,512]{2,1,0:T(8,128)(2,1)} %fusion.7), kind=kOutput, calls=%fused_computation.40 | convolution fusion | flops 1073741824 | bytes 5242880 | tf_op jit(solution)/shard_map/btv,btq->vq/dot_general | solution.py:116
  204.9 2.2 convolution_bitcast_fusion.3
  207.1 1.7 convolution_bitcast_fusion.1
  209.1 36.8 %all-reduce.7.cloned.1.call-done = (f32[512,512]{0,1:T(8,128)}, f32[512,512]{0,1:T(8,128)}, f32[512,512]{0,1:T(8,128)}) async-done(((f32[512,512]{0,1:T(8,128)}, f32[512,512]{0,1:T(8,128)}, f32[512,512]{0,1:T(8,128)}), (f32[512,512]{0,1:T(8,128)}, f32[512,512]{0,1:T(8,128)}, f32[512,512]{0,1:T(8,128)})) %all-reduce.7.cloned.1.call-update) | async-done | bytes 3145744 | tf_op jit(solution)/shard_map/psum | solution.py:60
  246.0 8.0 %fusion.10 = bf16[2,1024,512]{2,1,0:T(8,128)(2,1)} fusion(s32[1024]{0:T(1024)S(1)} %copy-done.14, f32[2,1024,512]{2,1,0:T(8,128)} %get-tuple-element.31, f32[2,1024,512]{2,1,0:T(8,128)} %copy-done.5), kind=kOutput, calls=%fused_computation.16 | convolution fusion | flops 2162163712 | bytes 10489856 | tf_op jit(solution)/shard_map/cn,scd->snd/dot_general | solution.py:34
  253.9 134.0 %all-reduce.5.cloned.1.call-done = (f32[512,512]{0,1:T(8,128)}, f32[512,512]{0,1:T(8,128)}, f32[512,512]{0,1:T(8,128)}) async-done(((f32[512,512]{0,1:T(8,128)}, f32[512,512]{0,1:T(8,128)}, f32[512,512]{0,1:T(8,128)}), (f32[512,512]{0,1:T(8,128)}, f32[512,512]{0,1:T(8,128)}, f32[512,512]{0,1:T(8,128)})) %all-reduce.5.cloned.1.call-update) | async-done | bytes 3145744 | tf_op jit(solution)/shard_map/psum | solution.py:60
  387.9 1.8 broadcast_multiply_fusion
  (50 shorter events, 13.9 us)
Async XLA Ops:
  7.2 29.9 %copy-start = (bf16[32,128,128]{2,1,0:T(8,128)(2,1)S(1)}, bf16[32,128,128]{2,1,0:T(8,128)(2,1)}, u32[]{:S(2)}) copy-start(bf16[32,128,128]{2,1,0:T(8,128)(2,1)} %param.12) | copy-start | bytes 3145732
  7.2 11.7 %copy-start.2 = (bf16[2,1024,512]{2,1,0:T(8,128)(2,1)S(1)}, bf16[2,1024,512]{2,1,0:T(8,128)(2,1)}, u32[]{:S(2)}) copy-start(bf16[2,1024,512]{2,1,0:T(8,128)(2,1)} %param.11) | copy-start | bytes 6291460
  7.2 238.7 %all-reduce.7.cloned.1.call-start = ((), (), s32[]{:S(2)}) async-start(), calls=%async_computation.1 | async-start | bytes 6291456 | tf_op jit(solution)/shard_map/psum | solution.py:60
  7.2 12.8 %copy-start.9 = (bf16[512,512]{1,0:T(8,128)(2,1)S(1)}, bf16[512,512]{1,0:T(8,128)(2,1)}, u32[]{:S(2)}) copy-start(bf16[512,512]{1,0:T(8,128)(2,1)} %param.19) | copy-start | bytes 1572868
  10.5 14.6 %collective-permute-start = (bf16[2,2,128,512]{3,1,2,0:T(2,128)(2,1)S(1)}, bf16[2,2,128,512]{3,1,2,0:T(2,128)(2,1)S(1)}, u32[]{:S(2)}, u32[]{:S(2)}) collective-permute-start(bf16[2,2,128,512]{3,1,2,0:T(2,128)(2,1)S(1)} %fusion.35), channel_id=1, source_target_pairs={{0,2},{2,4},{4,6},{6,8},{8,10},{10,12},{12,14},{14,16},{16,18},{18... | collective-permute-start | bytes 1572872 | tf_op jit(solution)/shard_map/ppermute | solution.py:11
  17.6 14.4 %collective-permute-start.1 = (bf16[2,2,128,512]{3,1,2,0:T(2,128)(2,1)S(1)}, bf16[2,2,128,512]{3,1,2,0:T(2,128)(2,1)S(1)}, u32[]{:S(2)}, u32[]{:S(2)}) collective-permute-start(bf16[2,2,128,512]{3,1,2,0:T(2,128)(2,1)S(1)} %fusion.36), channel_id=1, source_target_pairs={{2,0},{4,2},{6,4},{8,6},{10,8},{12,10},{14,12},{16,14},{18,16},{20... | collective-permute-start | bytes 1572872 | tf_op jit(solution)/shard_map/ppermute | solution.py:11
  20.1 11.9 %copy-start.15 = (s32[32]{0:T(128)S(1)}, s32[32]{0:T(128)}, u32[]{:S(2)}) copy-start(s32[32]{0:T(128)} %param.14) | copy-start | bytes 388
  55.6 20.0 %copy-start.11 = (s32[32]{0:T(128)S(1)}, s32[32]{0:T(128)}, u32[]{:S(2)}) copy-start(s32[32]{0:T(128)} %param.13) | copy-start | bytes 388
  75.6 11.6 %copy-start.10 = (bf16[512,512]{1,0:T(8,128)(2,1)S(1)}, bf16[512,512]{1,0:T(8,128)(2,1)}, u32[]{:S(2)}) copy-start(bf16[512,512]{1,0:T(8,128)(2,1)} %param.20) | copy-start | bytes 1572868
  85.2 2.9 copy-start.3
  85.9 1.3 copy-start.4
  88.1 1.3 copy-start.14
  89.4 5.5 %copy-start.5 = (f32[2,1024,512]{2,1,0:T(8,128)}, f32[2,1024,512]{2,1,0:T(8,128)S(1)}, u32[]{:S(2)}) copy-start(f32[2,1024,512]{2,1,0:T(8,128)S(1)} %convolution_add_fusion) | copy-start | bytes 12582916
  89.4 6.7 %copy-start.12 = (bf16[2,1024,512]{2,1,0:T(8,128)(2,1)S(1)}, bf16[2,1024,512]{2,1,0:T(8,128)(2,1)}, u32[]{:S(2)}) copy-start(bf16[2,1024,512]{2,1,0:T(8,128)(2,1)} %param.18) | copy-start | bytes 6291460
  94.9 45.6 %collective-permute-start.2 = (bf16[2,1024,512]{1,2,0:T(8,128)(2,1)}, bf16[2,1024,512]{1,2,0:T(8,128)(2,1)}, u32[]{:S(2)}, u32[]{:S(2)}) collective-permute-start(bf16[2,1024,512]{1,2,0:T(8,128)(2,1)} %get-tuple-element.26), channel_id=1, source_target_pairs={{0,2},{2,0},{4,6},{6,4},{8,10},{10,8},{12,14},{14,12},{16,18},{18,... | collective-permute-start | bytes 6291464 | tf_op jit(solution)/shard_map/ppermute | solution.py:17
  101.2 84.2 %collective-permute-start.3 = (bf16[2,1024,512]{2,1,0:T(8,128)(2,1)}, bf16[2,1024,512]{2,1,0:T(8,128)(2,1)}, u32[]{:S(2)}, u32[]{:S(2)}) collective-permute-start(bf16[2,1024,512]{2,1,0:T(8,128)(2,1)} %get-tuple-element.28), channel_id=1, source_target_pairs={{0,2},{2,0},{4,6},{6,4},{8,10},{10,8},{12,14},{14,12},{16,18},{18,... | collective-permute-start | bytes 6291464 | tf_op jit(solution)/shard_map/ppermute | solution.py:17
  140.4 44.9 %copy-start.13 = (bf16[512,512]{1,0:T(8,128)(2,1)S(1)}, bf16[512,512]{1,0:T(8,128)(2,1)}, u32[]{:S(2)}) copy-start(bf16[512,512]{1,0:T(8,128)(2,1)} %param.21) | copy-start | bytes 1572868
  140.4 44.9 %copy-start.17 = (f32[1024,2,512]{2,0,1:T(8,128)S(1)}, f32[1024,2,512]{2,0,1:T(8,128)}, u32[]{:S(2)}) copy-start(f32[1024,2,512]{2,0,1:T(8,128)} %get-tuple-element.29) | copy-start | bytes 12582916
  144.2 47.9 %copy-start.7 = (bf16[2,1024,512]{1,2,0:T(8,128)(2,1)}, bf16[2,1024,512]{1,2,0:T(8,128)(2,1)S(1)}, u32[]{:S(2)}) copy-start(bf16[2,1024,512]{1,2,0:T(8,128)(2,1)S(1)} %fusion.12) | copy-start | bytes 6291460
  200.2 4.6 %copy-start.6 = (bf16[2,1024,512]{2,1,0:T(8,128)(2,1)S(1)}, bf16[2,1024,512]{2,1,0:T(8,128)(2,1)}, u32[]{:S(2)}) copy-start(bf16[2,1024,512]{2,1,0:T(8,128)(2,1)} %fusion.7) | copy-start | bytes 6291460
  204.9 2.3 copy-start.8
  204.9 2.3 copy-start.16
  208.9 179.1 %all-reduce.5.cloned.1.call-start = ((), (), s32[]{:S(2)}) async-start(), calls=%async_computation | async-start | bytes 6291456 | tf_op jit(solution)/shard_map/psum | solution.py:60
  389.7 5.3 %copy-start.1 = (bf16[32,128,128]{2,1,0:T(8,128)(2,1)S(1)}, bf16[32,128,128]{2,1,0:T(8,128)(2,1)}, u32[]{:S(2)}) copy-start(bf16[32,128,128]{2,1,0:T(8,128)(2,1)} %param.12) | copy-start | bytes 3145732
Sparse Core Ops, SparseCore 0:
  209.0 36.8 all-reduce.6
  251.9 135.9 all-reduce.4
